TPU v7x, 32 devices: a whole 2x2x4 slice. The times are simulated.
32 devices in a mesh: ctx: 8 (over z, x), head: 4 (over y, core).
Axes of the slice: x: 2, y: 2, z: 4, core: 2. Of those that a mesh axis runs over, the one named last changes fastest.
Arguments:
- x_in: bfloat16 [8192, 4096], P('ctx', 'head'), may hold values from -6 to 6
- b_in: bfloat16 [8192, 128], P('ctx'), may hold values from -1.796875 to 1.796875
- c_in: bfloat16 [8192, 128], P('ctx'), may hold values from -1.796875 to 1.796875
- d_out: bfloat16 [8192, 4096], P('ctx', 'head'), may hold values from -0.75 to 0.75
- table: float32 [16, 18], replicated, may hold values from 0 to 3, as said below
- level_index: int32 [8192], P('ctx'), may hold values from 0 to 15
Outputs:
- y_out: bfloat16 [8192, 4096], P('ctx', 'head')
- dx_out: bfloat16 [8192, 4096], P('ctx', 'head')
- d_b: float32 [8192, 128], P(('ctx', 'head'))
- d_c: float32 [8192, 128], P(('ctx', 'head'))
Inputs may be any that keep to these rules, and one draw needn't show every extreme that they name: `table`: entries are positive.
All inputs are finite; a program needn't handle non-finite values.
Results may differ from a plain program's by a relative error of at most 0.006.
Values sent between devices are 32-bit elements; how exact they have to be, the bound alone decides.
A program may use at most 128 MiB of HBM per device.

v0:
```python
import jax
import jax.numpy as jnp
from jax import lax
from jax.sharding import PartitionSpec as P


def from_partner(block, axis, bit):
    count = lax.axis_size(axis)
    route = []
    for low in range(count):
        high = low | 1 << bit
        if high != low and high < count:
            route += [(low, high), (high, low)]
    return lax.ppermute(block, axis, route)


def bit_count(values, bits):
    counted = jnp.zeros(values.shape, jnp.int32)
    for digit_no in range(bits):
        counted = counted + (values >= 1 << digit_no).astype(jnp.int32)
    return counted


def local(x_in, b_in, c_in, d_out, table, level_index):
    tok_rows, feat_width = x_in.shape
    nstate = b_in.shape[1]
    low_bits = tok_rows.bit_length() - 1
    ctx_bits = lax.axis_size("ctx").bit_length() - 1
    my_block = lax.axis_index("ctx")
    table_rows = table.shape[0]
    chooser = (level_index[:, None] == jnp.arange(table_rows, dtype=jnp.int32)[None, :]).astype(
        jnp.float32
    )
    weights_tok = jnp.dot(chooser, table, precision=lax.Precision.HIGHEST)
    far_lam = weights_tok[:, low_bits + 1 : low_bits + 1 + ctx_bits]
    state = jnp.dot(b_in.T, x_in, preferred_element_type=jnp.float32)
    rising = (
        (far_lam[:, :, None] * c_in[:, None, :].astype(jnp.float32))
        .astype(jnp.bfloat16)
        .reshape(tok_rows, ctx_bits * nstate)
    )
    grad_state = jnp.dot(rising.T, d_out, preferred_element_type=jnp.float32).reshape(
        ctx_bits, nstate, feat_width
    )
    block_sum = state
    carry_parts = []
    for digit_no in range(ctx_bits):
        partner = from_partner(block_sum, "ctx", digit_no)
        upper_flag = (my_block >> digit_no & 1).astype(jnp.float32)
        carry_parts.append(partner * upper_flag)
        block_sum = block_sum + partner
    carry_full = jnp.stack(carry_parts)
    carry = carry_full.astype(jnp.bfloat16).reshape(ctx_bits * nstate, feat_width)
    pending = grad_state
    back_sum = jnp.zeros((nstate, feat_width), jnp.float32)
    for digit_no in range(ctx_bits):
        partner = from_partner(pending, "ctx", digit_no)
        lower_flag = (1 - (my_block >> digit_no & 1)).astype(jnp.float32)
        back_sum = back_sum + partner[0] * lower_flag
        pending = (pending + partner)[1:]
    back_state = back_sum.astype(jnp.bfloat16)
    block_rows = min(512, tok_rows)
    positions = jnp.arange(tok_rows, dtype=jnp.int32)
    y_parts = []
    c_parts = []
    dx_accum = jnp.zeros((tok_rows, feat_width), jnp.float32)
    grad_b = jnp.zeros((tok_rows, nstate), jnp.float32)
    for row_start in range(0, tok_rows, block_rows):
        row_stop = row_start + block_rows
        row_pos = positions[row_start:row_stop]
        col_pos = positions[:row_stop]
        level_map = bit_count(row_pos[:, None] ^ col_pos[None, :], low_bits)
        weight = jnp.zeros((block_rows, row_stop), jnp.float32)
        for level_no in range(low_bits + 1):
            weight = weight + jnp.where(
                level_map == level_no, weights_tok[row_start:row_stop, level_no][:, None], 0.0
            )
        weight = jnp.where(col_pos[None, :] <= row_pos[:, None], weight, 0.0)
        scores = jnp.dot(
            c_in[row_start:row_stop], b_in[:row_stop].T, preferred_element_type=jnp.float32
        )
        mixing = (scores * weight).astype(jnp.bfloat16)
        y_rows = jnp.dot(mixing, x_in[:row_stop], preferred_element_type=jnp.float32) + jnp.dot(
            rising[row_start:row_stop], carry, preferred_element_type=jnp.float32
        )
        y_parts.append(y_rows.astype(jnp.bfloat16))
        dx_accum = dx_accum.at[:row_stop].add(
            jnp.dot(mixing.T, d_out[row_start:row_stop], preferred_element_type=jnp.float32)
        )
        d_mix = (
            jnp.dot(
                d_out[row_start:row_stop], x_in[:row_stop].T, preferred_element_type=jnp.float32
            )
            * weight
        ).astype(jnp.bfloat16)
        c_parts.append(jnp.dot(d_mix, b_in[:row_stop], preferred_element_type=jnp.float32))
        grad_b = grad_b.at[:row_stop].add(
            jnp.dot(d_mix.T, c_in[row_start:row_stop], preferred_element_type=jnp.float32)
        )
    y_out = jnp.concatenate(y_parts, axis=0)
    dx_out = (dx_accum + jnp.dot(b_in, back_state, preferred_element_type=jnp.float32)).astype(
        jnp.bfloat16
    )
    far_terms = jnp.dot(d_out, carry.T, preferred_element_type=jnp.float32).reshape(
        tok_rows, ctx_bits, nstate
    )
    grad_c = jnp.concatenate(c_parts, axis=0) + jnp.sum(far_terms * far_lam[:, :, None], axis=1)
    grad_b = grad_b + jnp.dot(x_in, back_state.T, preferred_element_type=jnp.float32)
    d_b, d_c = (
        lax.psum_scatter(grad_b, "head", scatter_dimension=0, tiled=True),
        lax.psum_scatter(grad_c, "head", scatter_dimension=0, tiled=True),
    )
    return (y_out, dx_out, d_b, d_c)


def solution(mesh):
    return jax.shard_map(
        local,
        mesh=mesh,
        in_specs=(
            P("ctx", "head"),
            P("ctx", None),
            P("ctx", None),
            P("ctx", "head"),
            P(),
            P("ctx"),
        ),
        out_specs=(
            P("ctx", "head"),
            P("ctx", "head"),
            P(("ctx", "head"), None),
            P(("ctx", "head"), None),
        ),
        check_vma=False,
    )
```

profile of v0, /device:TPU:0, one launch (start us, length us, event | category | flops | bytes accessed | tf_op | source)
XLA Modules:
  0.0 197.3 jit_solution(562153425174783089)
XLA Ops:
  7.2 0.0 copy-start
  7.2 0.0 reduce-scatter.5.cloned.1.call-start
  7.2 2.3 %fusion.46 = f32[128,1024]{1,0:T(8,128)S(1)} fusion(bf16[1024,128]{1,0:T(8,128)(2,1)} %param.19, bf16[1024,1024]{1,0:T(8,128)(2,1)} %param.18), kind=kOutput, calls=%fused_computation.84 | convolution fusion | flops 268435456 | bytes 2883584 | tf_op jit(solution)/shard_map/dot_general | solution.py:36
  9.5 3.0 %collective-permute-start = (f32[128,1024]{1,0:T(8,128)S(1)}, f32[128,1024]{1,0:T(8,128)S(1)}, u32[]{:S(2)}, u32[]{:S(2)}) collective-permute-start(f32[128,1024]{1,0:T(8,128)S(1)} %fusion.46), channel_id=1, source_target_pairs={{0,4},{4,0},{8,12},{12,8},{16,20},{20,16},{24,28},{28,24},{1,5},{5... | collective-permute-start | bytes 1572872 | tf_op jit(solution)/shard_map/ppermute | solution.py:14
  12.6 0.5 fusion.31
  13.1 0.0 copy-done.2
  13.1 0.0 copy-start.10
  13.1 0.0 copy-start.21
  13.1 7.6 %multiply_convert_fusion = bf16[512,1024]{1,0:T(8,128)(2,1)} fusion(bf16[1024,1024]{1,0:T(8,128)(2,1)S(1)} %copy-done.2, f32[512]{0:T(512)S(1)} %bitcast.97, f32[512]{0:T(512)S(1)} %bitcast.99, f32[512]{0:T(512)S(1)} %bitcast.101, f32[512]{0:T(512)S(1)} %bitcast.103, f32[512]{0:T(512)S(1)} %bitcast.105, f32[512]{0:T(512)S(1)} %bitcast.107, ...), kind=kOutput, calls=%fused_computation.19 | convolution fusion | flops 1108344832 | bytes 4218880 | tf_op jit(solution)/shard_map/dot_general | solution.py:91
  20.7 3.8 %collective-permute-done = f32[128,1024]{1,0:T(8,128)S(1)} collective-permute-done((f32[128,1024]{1,0:T(8,128)S(1)}, f32[128,1024]{1,0:T(8,128)S(1)}, u32[]{:S(2)}, u32[]{:S(2)}) %collective-permute-start) | collective-permute-done | bytes 524320 | tf_op jit(solution)/shard_map/ppermute | solution.py:14
  24.5 0.1 add.564
  24.6 1.9 collective-permute-start.1
  26.5 2.6 %fusion.15 = bf16[512,512]{1,0:T(8,128)(2,1)S(1)} fusion(f32[512]{0:T(512)S(1)} %bitcast.83, f32[512]{0:T(512)S(1)} %bitcast.85, f32[512]{0:T(512)S(1)} %bitcast.87, f32[512]{0:T(512)S(1)} %bitcast.89, f32[512]{0:T(512)S(1)} %bitcast.91, f32[512]{0:T(512)S(1)} %bitcast.93, f32[512]{0:T(512)S(1)} %bitcast.95, f32[512]{0:T(512)S(1)} %bitcast.121, ...), kind=kOutput, calls=%fused_computation.40 | convolution fusion | flops 84410368 | bytes 813056 | tf_op jit(solution)/shard_map/dot_general | solution.py:79
  29.1 0.0 copy-done.17
  29.1 2.1 %fusion.22 = f32[512,1024]{1,0:T(8,128)} fusion(bf16[512,512]{1,0:T(8,128)(2,1)S(1)} %fusion.15, bf16[1024,1024]{1,0:T(8,128)(2,1)S(1)} %copy-done.17), kind=kOutput, calls=%fused_computation.52 | convolution fusion | flops 536870912 | bytes 3670016 | tf_op jit(solution)/shard_map/dot_general | solution.py:88
  31.2 6.5 %collective-permute-done.1 = f32[128,1024]{1,0:T(8,128)S(1)} collective-permute-done((f32[128,1024]{1,0:T(8,128)S(1)}, f32[128,1024]{1,0:T(8,128)S(1)}, u32[]{:S(2)}, u32[]{:S(2)}) %collective-permute-start.1) | collective-permute-done | bytes 524320 | tf_op jit(solution)/shard_map/ppermute | solution.py:14
  37.7 0.9 add.565
  38.6 2.6 %collective-permute-start.2 = (f32[128,1024]{1,0:T(8,128)}, f32[128,1024]{1,0:T(8,128)}, u32[]{:S(2)}, u32[]{:S(2)}) collective-permute-start(f32[128,1024]{1,0:T(8,128)} %add.565), channel_id=1, source_target_pairs={{0,16},{16,0},{4,20},{20,4},{8,24},{24,8},{12,28},{28,12},{1,17},{... | collective-permute-start | bytes 1572872 | tf_op jit(solution)/shard_map/ppermute | solution.py:14
  41.2 2.0 %fusion.25 = f32[512,1024]{1,0:T(8,128)} fusion(bf16[512,512]{1,0:T(8,128)(2,1)S(1)} %fusion.15, bf16[1024,1024]{1,0:T(8,128)(2,1)S(1)} %copy-done.2), kind=kOutput, calls=%fused_computation.55 | convolution fusion | flops 536870912 | bytes 3670016 | tf_op jit(solution)/shard_map/dot_general | solution.py:83
  43.2 0.9 convert_element_type.535
  44.1 1.2 multiply_bitcast_fusion.1
  45.4 18.0 %collective-permute-done.2 = f32[128,1024]{1,0:T(8,128)} collective-permute-done((f32[128,1024]{1,0:T(8,128)}, f32[128,1024]{1,0:T(8,128)}, u32[]{:S(2)}, u32[]{:S(2)}) %collective-permute-start.2) | collective-permute-done | bytes 524320 | tf_op jit(solution)/shard_map/ppermute | solution.py:14
  63.3 1.1 multiply_bitcast_fusion
  64.4 0.0 copy-start.7
  64.4 0.7 copy-done.7
  65.1 0.1 maximum_convert_fusion
  65.2 0.0 copy-done.18
  65.2 2.2 %fusion.49 = f32[384,1024]{1,0:T(8,128)} fusion(bf16[384,1024]{1,0:T(8,128)(2,1)S(1)} %bitcast.80, bf16[1024,1024]{1,0:T(8,128)(2,1)S(1)} %copy-done.18), kind=kOutput, calls=%fused_computation.87 | convolution fusion | flops 805306368 | bytes 4456448 | tf_op jit(solution)/shard_map/dot_general | solution.py:104
  67.4 3.1 %copy.15 = f32[1024,3,128]{2,0,1:T(8,128)} copy(f32[1024,3,128]{0,2,1:T(8,128)} %bitcast.79) | data formatting | bytes 3145728 | tf_op jit(solution)/shard_map/reshape | solution.py:104
  70.5 2.8 %multiply_reduce_fusion = (f32[1024,128]{1,0:T(8,128)}, bf16[1024,3,128]{2,0,1:T(8,128)(2,1)S(1)}) fusion(f32[1024,3,128]{2,0,1:T(8,128)} %copy.15, f32[1024,3]{0,1:T(4,128)S(1)} %slice.272, f32[1024,128]{1,0:T(8,128)} %convert_element_type.535), kind=kLoop, calls=%fused_computation.36 | loop fusion | flops 1441792 | bytes 3420160 | tf_op jit(solution)/shard_map/reduce_sum | solution.py:107
  73.3 1.2 copy.12
  74.5 2.9 %fusion.1 = f32[3,128,1024]{2,1,0:T(8,128)S(1)} fusion(bf16[1024,1024]{1,0:T(8,128)(2,1)} %param.21, bf16[1024,3,128]{0,2,1:T(8,128)(2,1)} %copy.12), kind=kOutput, calls=%fused_computation.13 | convolution fusion | flops 805306368 | bytes 4456448 | tf_op jit(solution)/shard_map/dot_general | solution.py:42
  77.4 1.2 collective-permute-start.3
  78.7 1.2 fusion.48
  79.8 5.2 %multiply_convert_fusion.1 = bf16[512,1024]{1,0:T(8,128)(2,1)S(1)} fusion(bf16[1024,128]{1,0:T(8,128)(2,1)S(1)} %copy-done.11, f32[512]{0:T(512)S(1)} %bitcast.98, f32[512]{0:T(512)S(1)} %bitcast.100, f32[512]{0:T(512)S(1)} %bitcast.102, f32[512]{0:T(512)S(1)} %bitcast.104, f32[512]{0:T(512)S(1)} %bitcast.106, f32[512]{0:T(512)S(1)} %bitcast.108, ...), kind=kOutput, calls=%fused_computation.20 | convolution fusion | flops 168820736 | bytes 1466368 | tf_op jit(solution)/shard_map/dot_general | solution.py:79
  85.1 3.3 %fusion.19 = f32[1024,1024]{1,0:T(8,128)} fusion(bf16[512,1024]{1,0:T(8,128)(2,1)S(1)} %multiply_convert_fusion.1, bf16[1024,1024]{1,0:T(8,128)(2,1)S(1)} %copy-done.19), kind=kOutput, calls=%fused_computation.49 | convolution fusion | flops 1073741824 | bytes 6291456 | tf_op jit(solution)/shard_map/dot_general | solution.py:88
  88.3 24.8 %collective-permute-done.3 = f32[3,128,1024]{2,1,0:T(8,128)S(1)} collective-permute-done((f32[3,128,1024]{2,1,0:T(8,128)S(1)}, f32[3,128,1024]{2,1,0:T(8,128)S(1)}, u32[]{:S(2)}, u32[]{:S(2)}) %collective-permute-start.3) | collective-permute-done | bytes 1572896 | tf_op jit(solution)/shard_map/ppermute | solution.py:14
  113.1 0.2 slice_add_fusion
  113.3 1.1 collective-permute-start.4
  114.4 2.6 %fusion.47 = f32[512,1024]{1,0:T(8,128)} fusion(bf16[512,1024]{1,0:T(8,128)(2,1)S(1)} %multiply_convert_fusion.1, bf16[1024,1024]{1,0:T(8,128)(2,1)S(1)} %copy-done.2), kind=kOutput, calls=%fused_computation.85 | convolution fusion | flops 1073741824 | bytes 5242880 | tf_op jit(solution)/shard_map/dot_general | solution.py:83
  117.0 2.7 %fusion.16 = bf16[512,512]{1,0:T(8,128)(2,1)S(1)} fusion(bf16[1024,1024]{1,0:T(8,128)(2,1)S(1)} %copy-done.19, bf16[1024,1024]{1,0:T(8,128)(2,1)S(1)} %copy-done.2, f32[512]{0:T(512)S(1)} %bitcast.84, f32[512]{0:T(512)S(1)} %bitcast.86, f32[512]{0:T(512)S(1)} %bitcast.88, f32[512]{0:T(512)S(1)} %bitcast.90, f32[512]{0:T(512)S(1)} %bitcast.92, ...), kind=kOutput, calls=%fused_computation.41 | convolution fusion | flops 554172416 | bytes 2648064 | tf_op jit(solution)/shard_map/dot_general | solution.py:91
  119.7 17.2 %collective-permute-done.4 = f32[2,128,1024]{2,1,0:T(8,128)S(1)} collective-permute-done((f32[2,128,1024]{2,1,0:T(8,128)S(1)}, f32[2,128,1024]{2,1,0:T(8,128)S(1)}, u32[]{:S(2)}, u32[]{:S(2)}) %collective-permute-start.4) | collective-permute-done | bytes 1048608 | tf_op jit(solution)/shard_map/ppermute | solution.py:14
  136.9 1.0 slice_add_fusion.1
  137.9 0.2 copy-done.24
  138.0 3.4 %collective-permute-start.5 = (f32[1,128,1024]{2,1,0:T(8,128)}, f32[1,128,1024]{2,1,0:T(8,128)}, u32[]{:S(2)}, u32[]{:S(2)}) collective-permute-start(f32[1,128,1024]{2,1,0:T(8,128)} %slice_add_fusion.1), channel_id=1, source_target_pairs={{0,16},{16,0},{4,20},{20,4},{8,24},{24,8},{12,28},{28,12},{1,17},{... | collective-permute-start | bytes 1572872 | tf_op jit(solution)/shard_map/ppermute | solution.py:14
  141.4 1.0 fusion.38
  142.4 2.1 %maximum_add_fusion = f32[1024,128]{1,0:T(8,128)} fusion(f32[1024,128]{1,0:T(8,128)} %get-tuple-element.90, f32[512,128]{1,0:T(8,128)} %fusion.48, f32[512,128]{1,0:T(8,128)} %fusion.38), kind=kLoop, calls=%fused_computation.64 | loop fusion | flops 262144 | bytes 1572864 | tf_op jit(solution)/shard_map/add | solution.py:107
  144.5 0.0 reduce-scatter.5.cloned.1.call-update
  144.5 0.0 reduce-scatter.3.cloned.1.call-start
  144.5 1.4 fusion.41
  146.0 0.0 copy-start.23
  146.0 17.7 %collective-permute-done.5 = f32[1,128,1024]{2,1,0:T(8,128)} collective-permute-done((f32[1,128,1024]{2,1,0:T(8,128)}, f32[1,128,1024]{2,1,0:T(8,128)}, u32[]{:S(2)}, u32[]{:S(2)}) %collective-permute-start.5) | collective-permute-done | bytes 524320 | tf_op jit(solution)/shard_map/ppermute | solution.py:14
  163.6 1.5 fusion.34
  165.1 0.7 convolution_bitcast_fusion
  165.9 1.3 fusion.17
  167.2 0.0 reduce-scatter.3.cloned.1.call-update
  167.2 0.0 copy-start.4
  167.2 2.5 %fusion.3 = bf16[512,1024]{1,0:T(8,128)(2,1)S(1)} fusion(f32[512,1024]{1,0:T(8,128)} %fusion.47, bf16[1024,3,128]{2,0,1:T(8,128)(2,1)S(1)} %get-tuple-element.91, bf16[1,128,1024]{2,1,0:T(8,128)(2,1)S(1)} %copy-done.8, bf16[1,128,1024]{2,1,0:T(8,128)(2,1)S(1)} %multiply_bitcast_fusion.1, bf16[1,128,1024]{2,1,0:T(8,128)(2,1)S(1)} %multiply_bitcast_fusion.2), kind=kOutput, calls=%fused_computation.16 | convolution fusion | flops 404488192 | bytes 4325376 | tf_op jit(solution)/shard_map/dot_general | solution.py:83
  169.8 0.0 copy-start.12
  169.8 0.7 fusion.4
  170.5 1.5 pad_maximum_fusion
  172.0 1.7 copy-done.1
  173.7 2.0 %fusion = bf16[1024,1024]{1,0:T(8,128)(2,1)} fusion(f32[1024,1024]{1,0:T(8,128)S(1)} %copy-done.1, f32[512,1024]{1,0:T(8,128)S(1)} %copy-done.3, bf16[1024,128]{1,0:T(8,128)(2,1)S(1)} %copy-done.12, bf16[128,1024]{1,0:T(8,128)(2,1)S(1)} %copy-done.14), kind=kOutput, calls=%fused_computation.11 | convolution fusion | flops 271581184 | bytes 8912896 | tf_op jit(solution)/shard_map/dot_general | solution.py:101
  175.7 14.7 %reduce-scatter.3.cloned.1.call-done = f32[256,128]{1,0:T(8,128)} async-done(((f32[1024,128]{1,0:T(8,128)}), f32[256,128]{1,0:T(8,128)}) %reduce-scatter.3.cloned.1.call-update) | async-done | bytes 131088 | tf_op jit(solution)/shard_map/reduce_scatter | solution.py:110
  (48 shorter events, 0.2 us)
Async XLA Ops:
  7.2 5.4 %copy-start = (f32[16,18]{1,0:T(8,128)S(1)}, f32[16,18]{1,0:T(8,128)}, u32[]{:S(2)}) copy-start(f32[16,18]{1,0:T(8,128)} %param.22) | copy-start | bytes 3460
  7.2 5.9 %copy-start.2 = (bf16[1024,1024]{1,0:T(8,128)(2,1)S(1)}, bf16[1024,1024]{1,0:T(8,128)(2,1)}, u32[]{:S(2)}) copy-start(bf16[1024,1024]{1,0:T(8,128)(2,1)} %param.18) | copy-start | bytes 6291460
  7.2 5.4 %copy-start.25 = (s32[1024]{0:T(1024)S(1)}, s32[1024]{0:T(1024)}, u32[]{:S(2)}) copy-start(s32[1024]{0:T(1024)} %param.23) | copy-start | bytes 12292
  7.2 168.5 %reduce-scatter.5.cloned.1.call-start = ((), (), s32[]{:S(2)}) async-start(), calls=%async_computation.3 | async-start | bytes 655360 | tf_op jit(solution)/shard_map/reduce_scatter | solution.py:111
  9.5 15.0 %collective-permute-start = (f32[128,1024]{1,0:T(8,128)S(1)}, f32[128,1024]{1,0:T(8,128)S(1)}, u32[]{:S(2)}, u32[]{:S(2)}) collective-permute-start(f32[128,1024]{1,0:T(8,128)S(1)} %fusion.46), channel_id=1, source_target_pairs={{0,4},{4,0},{8,12},{12,8},{16,20},{20,16},{24,28},{28,24},{1,5},{5... | collective-permute-start | bytes 1572872 | tf_op jit(solution)/shard_map/ppermute | solution.py:14
  13.1 13.3 %copy-start.10 = (bf16[1024,128]{1,0:T(8,128)(2,1)S(1)}, bf16[1024,128]{1,0:T(8,128)(2,1)}, u32[]{:S(2)}) copy-start(bf16[1024,128]{1,0:T(8,128)(2,1)} %param.19) | copy-start | bytes 786436
  13.1 13.3 %copy-start.21 = (bf16[1024,128]{1,0:T(8,128)(2,1)S(1)}, bf16[1024,128]{1,0:T(8,128)(2,1)}, u32[]{:S(2)}) copy-start(bf16[1024,128]{1,0:T(8,128)(2,1)} %param.20) | copy-start | bytes 786436
  24.6 13.2 %collective-permute-start.1 = (f32[128,1024]{1,0:T(8,128)S(1)}, f32[128,1024]{1,0:T(8,128)S(1)}, u32[]{:S(2)}, u32[]{:S(2)}) collective-permute-start(f32[128,1024]{1,0:T(8,128)S(1)} %add.564), channel_id=1, source_target_pairs={{0,8},{8,0},{4,12},{12,4},{16,24},{24,16},{20,28},{28,20},{1,9},{9... | collective-permute-start | bytes 1572872 | tf_op jit(solution)/shard_map/ppermute | solution.py:14
  26.5 2.6 %copy-start.17 = (bf16[1024,1024]{1,0:T(8,128)(2,1)S(1)}, bf16[1024,1024]{1,0:T(8,128)(2,1)}, u32[]{:S(2)}) copy-start(bf16[1024,1024]{1,0:T(8,128)(2,1)} %param.21) | copy-start | bytes 6291460
  37.7 5.5 %copy-start.16 = (f32[128,1024]{1,0:T(8,128)}, f32[128,1024]{1,0:T(8,128)S(1)}, u32[]{:S(2)}) copy-start(f32[128,1024]{1,0:T(8,128)S(1)} %collective-permute-done.1) | copy-start | bytes 1572868
  38.6 24.7 %collective-permute-start.2 = (f32[128,1024]{1,0:T(8,128)}, f32[128,1024]{1,0:T(8,128)}, u32[]{:S(2)}, u32[]{:S(2)}) collective-permute-start(f32[128,1024]{1,0:T(8,128)} %add.565), channel_id=1, source_target_pairs={{0,16},{16,0},{4,20},{20,4},{8,24},{24,8},{12,28},{28,12},{1,17},{... | collective-permute-start | bytes 1572872 | tf_op jit(solution)/shard_map/ppermute | solution.py:14
  44.1 21.1 %copy-start.18 = (bf16[1024,1024]{1,0:T(8,128)(2,1)S(1)}, bf16[1024,1024]{1,0:T(8,128)(2,1)}, u32[]{:S(2)}) copy-start(bf16[1024,1024]{1,0:T(8,128)(2,1)} %param.21) | copy-start | bytes 6291460
  64.4 0.7 copy-start.7
  74.5 4.2 %copy-start.5 = (bf16[512,1024]{1,0:T(8,128)(2,1)S(1)}, bf16[512,1024]{1,0:T(8,128)(2,1)}, u32[]{:S(2)}) copy-start(bf16[512,1024]{1,0:T(8,128)(2,1)} %multiply_convert_fusion) | copy-start | bytes 3145732
  74.5 4.2 %copy-start.11 = (bf16[1024,128]{1,0:T(8,128)(2,1)S(1)}, bf16[1024,128]{1,0:T(8,128)(2,1)}, u32[]{:S(2)}) copy-start(bf16[1024,128]{1,0:T(8,128)(2,1)} %param.19) | copy-start | bytes 786436
  74.5 5.3 %copy-start.22 = (bf16[1024,128]{1,0:T(8,128)(2,1)S(1)}, bf16[1024,128]{1,0:T(8,128)(2,1)}, u32[]{:S(2)}) copy-start(bf16[1024,128]{1,0:T(8,128)(2,1)} %param.20) | copy-start | bytes 786436
  77.4 35.7 %collective-permute-start.3 = (f32[3,128,1024]{2,1,0:T(8,128)S(1)}, f32[3,128,1024]{2,1,0:T(8,128)S(1)}, u32[]{:S(2)}, u32[]{:S(2)}) collective-permute-start(f32[3,128,1024]{2,1,0:T(8,128)S(1)} %fusion.1), channel_id=1, source_target_pairs={{0,4},{4,0},{8,12},{12,8},{16,20},{20,16},{24,28},{28,24},{1,5},{5... | collective-permute-start | bytes 4718600 | tf_op jit(solution)/shard_map/ppermute | solution.py:14
  79.8 5.2 %copy-start.19 = (bf16[1024,1024]{1,0:T(8,128)(2,1)S(1)}, bf16[1024,1024]{1,0:T(8,128)(2,1)}, u32[]{:S(2)}) copy-start(bf16[1024,1024]{1,0:T(8,128)(2,1)} %param.21) | copy-start | bytes 6291460
  113.1 3.9 %copy-start.20 = (f32[3,128,1024]{2,1,0:T(8,128)}, f32[3,128,1024]{2,1,0:T(8,128)S(1)}, u32[]{:S(2)}) copy-start(f32[3,128,1024]{2,1,0:T(8,128)S(1)} %collective-permute-done.3) | copy-start | bytes 4718596
  113.3 23.6 %collective-permute-start.4 = (f32[2,128,1024]{2,1,0:T(8,128)S(1)}, f32[2,128,1024]{2,1,0:T(8,128)S(1)}, u32[]{:S(2)}, u32[]{:S(2)}) collective-permute-start(f32[2,128,1024]{2,1,0:T(8,128)S(1)} %slice_add_fusion), channel_id=1, source_target_pairs={{0,8},{8,0},{4,12},{12,4},{16,24},{24,16},{20,28},{28,20},{1,9},{9... | collective-permute-start | bytes 3145736 | tf_op jit(solution)/shard_map/ppermute | solution.py:14
  119.7 21.7 %copy-start.15 = (bf16[512,512]{1,0:T(8,128)(2,1)}, bf16[512,512]{1,0:T(8,128)(2,1)S(1)}, u32[]{:S(2)}) copy-start(bf16[512,512]{1,0:T(8,128)(2,1)S(1)} %fusion.16) | copy-start | bytes 1572868
  136.9 1.1 copy-start.24
  138.0 25.6 %collective-permute-start.5 = (f32[1,128,1024]{2,1,0:T(8,128)}, f32[1,128,1024]{2,1,0:T(8,128)}, u32[]{:S(2)}, u32[]{:S(2)}) collective-permute-start(f32[1,128,1024]{2,1,0:T(8,128)} %slice_add_fusion.1), channel_id=1, source_target_pairs={{0,16},{16,0},{4,20},{20,4},{8,24},{24,8},{12,28},{28,12},{1,17},{... | collective-permute-start | bytes 1572872 | tf_op jit(solution)/shard_map/ppermute | solution.py:14
  144.5 45.9 %reduce-scatter.3.cloned.1.call-start = ((), (), s32[]{:S(2)}) async-start(), calls=%async_computation.2 | async-start | bytes 655360 | tf_op jit(solution)/shard_map/reduce_scatter | solution.py:110
  145.9 19.9 %copy-start.6 = (bf16[512,1024]{1,0:T(8,128)(2,1)S(1)}, bf16[512,1024]{1,0:T(8,128)(2,1)}, u32[]{:S(2)}) copy-start(bf16[512,1024]{1,0:T(8,128)(2,1)} %multiply_convert_fusion) | copy-start | bytes 3145732
  146.0 19.9 %copy-start.23 = (bf16[1024,128]{1,0:T(8,128)(2,1)S(1)}, bf16[1024,128]{1,0:T(8,128)(2,1)}, u32[]{:S(2)}) copy-start(bf16[1024,128]{1,0:T(8,128)(2,1)} %param.20) | copy-start | bytes 786436
  165.1 0.7 copy-start.13
  165.9 1.3 copy-start.8
  167.2 2.5 %copy-start.4 = (f32[512,1024]{1,0:T(8,128)S(1)}, f32[512,1024]{1,0:T(8,128)}, u32[]{:S(2)}) copy-start(f32[512,1024]{1,0:T(8,128)} %fusion.25) | copy-start | bytes 6291460
  167.2 2.5 %copy-start.9 = (bf16[1,128,1024]{2,1,0:T(8,128)(2,1)S(1)}, bf16[1,128,1024]{2,1,0:T(8,128)(2,1)}, u32[]{:S(2)}) copy-start(bf16[1,128,1024]{2,1,0:T(8,128)(2,1)} %copy-done.7) | copy-start | bytes 786436
  169.7 2.3 %copy-start.3 = (f32[512,1024]{1,0:T(8,128)S(1)}, f32[512,1024]{1,0:T(8,128)}, u32[]{:S(2)}) copy-start(f32[512,1024]{1,0:T(8,128)} %fusion.22) | copy-start | bytes 6291460
  169.8 2.3 %copy-start.12 = (bf16[1024,128]{1,0:T(8,128)(2,1)S(1)}, bf16[1024,128]{1,0:T(8,128)(2,1)}, u32[]{:S(2)}) copy-start(bf16[1024,128]{1,0:T(8,128)(2,1)} %param.19) | copy-start | bytes 786436
  169.8 2.3 %copy-start.14 = (bf16[128,1024]{1,0:T(8,128)(2,1)S(1)}, bf16[128,1024]{1,0:T(8,128)(2,1)}, u32[]{:S(2)}) copy-start(bf16[128,1024]{1,0:T(8,128)(2,1)} %copy-done.13) | copy-start | bytes 786436
  170.5 3.2 %copy-start.1 = (f32[1024,1024]{1,0:T(8,128)S(1)}, f32[1024,1024]{1,0:T(8,128)}, u32[]{:S(2)}) copy-start(f32[1024,1024]{1,0:T(8,128)} %fusion.19) | copy-start | bytes 12582916
Sparse Core Ops, SparseCore 0:
  144.6 21.0 reduce-scatter.4
  168.8 21.6 reduce-scatter.2
where the time goes:
time: 198 us; the launch traced here: 197 us
  waiting for transfers between devices  103 us (52%)
  matrix products  46.6 us (24%)
  between operations  14.4 us (7%)
  starting transfers between devices  13.3 us (7%)
  other arithmetic  13.3 us (7%)
  local copies, waits for them, and re-layouts  6.94 us (4%)
    ppermute x6, waiting for transfers between devices, from_partner(): return lax.ppermute(block, axis, route)  87.9 us
    reduce_scatter x1, waiting for transfers between devices, local(): lax.psum_scatter(grad_b, 'head', scatter_dimension=0, tiled=True)  14.7 us
    ppermute x6, starting transfers between devices, from_partner(): return lax.ppermute(block, axis, route)  13.2 us
    dot_general x2, matrix products, local(): jnp.dot(d_out[row_start:row_stop], x_in[:row_stop].T, preferred_element_t...  10.2 us
    dot_general x2, matrix products, local(): jnp.dot(c_in[row_start:row_stop], b_in[:row_stop].T, preferred_element_ty...  7.85 us
    dot_general x2, matrix products, local(): jnp.dot(mixing.T, d_out[row_start:row_stop], preferred_element_type=jnp.f...  5.35 us
    dot_general x2, matrix products, local(): jnp.dot(mixing, x_in[:row_stop], preferred_element_type=jnp.float32)  4.63 us
  transfers between devices with their start and end apart: 8, of which 7 were waited for; matrix products, arithmetic and copies ran while one was open for 24% of the time, Pallas kernels for 0%

commit v1 on v0

v1 whole, which is shorter than its diff:
```python
import functools

import jax
import jax.numpy as jnp
from jax import lax
from jax.experimental import pallas as pl
from jax.experimental.pallas import tpu as pltpu
from jax.sharding import PartitionSpec as P

F32 = jnp.float32
BF16 = jnp.bfloat16
MESH = pl.DeviceIdType.MESH
TILE = 256
WIDTH = 256


def mm(a, b):
    return jnp.dot(a, b, preferred_element_type=F32)


def mm_tn(a, b):
    return lax.dot_general(a, b, (((0,), (0,)), ((), ())), preferred_element_type=F32)


def mm_nt(a, b):
    return lax.dot_general(a, b, (((1,), (1,)), ((), ())), preferred_element_type=F32)


def bit_count(values, bits):
    counted = jnp.zeros(values.shape, jnp.int32)
    for digit_no in range(bits):
        counted = counted + (values >= 1 << digit_no).astype(jnp.int32)
    return counted


def kernel(
    count,
    heads,
    x_ref,
    b_ref,
    c_ref,
    d_ref,
    w_ref,
    far_t_ref,
    y_ref,
    dx_ref,
    db_ref,
    dc_ref,
    y_acc,
    dx_acc,
    grads,
    rise,
    rise_t,
    carry,
    s_buf,
    g_buf,
    rx0,
    up,
    rc,
    rb,
    tot,
    xb,
    rxb,
    *rest,
):
    bits = count.bit_length() - 1
    head_bits = heads.bit_length() - 1
    r_in = rest[:head_bits]
    r_out = rest[head_bits : 2 * head_bits - 1]
    sems = rest[2 * head_bits - 1 :]
    (x0_s, x0_r, up_s, rc_r, bk_s, rb_r, xb_s, xb_r), hd_sems = sems[:8], sems[8:]
    toks, feats = x_ref.shape
    nstate = b_ref.shape[1]
    chunks = feats // WIDTH
    blocks = toks // TILE
    tile_bits = TILE.bit_length() - 1
    low_bits = toks.bit_length() - 1
    me = lax.axis_index("ctx")
    head = lax.axis_index("head")
    par = me % 2
    col = me // 2
    levels = range(1, bits)
    top = {k: col % (1 << k) == (1 << (k - 1)) - 1 for k in levels}
    is_set = {k: (me // (1 << k)) % 2 == 1 for k in range(bits)}
    last = col == count // 2 - 1
    late = {
        k: is_set[k] & ((col % (1 << k) != (1 << k) - 1) | last) for k in levels
    }

    barrier = pltpu.get_barrier_semaphore()
    for off in range(1, count):
        pl.semaphore_signal(
            barrier, inc=1, device_id={"ctx": (me + off) % count}, device_id_type=MESH
        )
    for off in range(1, heads):
        pl.semaphore_signal(
            barrier, inc=1, device_id={"head": (head + off) % heads}, device_id_type=MESH
        )

    def remote(src, dst, ssem, rsem, device):
        return pltpu.make_async_remote_copy(
            src_ref=src,
            dst_ref=dst,
            send_sem=ssem,
            recv_sem=rsem,
            device_id=device,
            device_id_type=MESH,
        )

    partner = me + 1 - 2 * par

    def x0_copy(q):
        return remote(s_buf.at[q], rx0.at[q], x0_s.at[q], x0_r.at[q], {"ctx": partner})

    def up_copy(k, step, q):
        return remote(
            up.at[q],
            rc.at[k - 1, q],
            up_s.at[step, q],
            rc_r.at[k - 1, q],
            {"ctx": (me + 2 + 2 * step) % count},
        )

    def back_copy(k, q):
        step = (me % (1 << k)) // 2
        dest = (me // (2 << k)) * (2 << k) + (1 << k) - 2 + par
        return remote(
            g_buf.at[k, q], rb.at[step, q], bk_s.at[k - 1, q], rb_r.at[step, q], {"ctx": dest}
        )

    def rb_wait(step, q):
        remote(
            g_buf.at[0, q], rb.at[step, q], bk_s.at[0, q], rb_r.at[step, q], {"ctx": partner}
        ).wait_recv()

    def xb_copy(q):
        return remote(xb.at[q], rxb.at[q], xb_s.at[q], xb_r.at[q], {"ctx": partner})

    b_t = b_ref[...].astype(F32).T.astype(BF16)
    c_f = c_ref[...].astype(F32)
    c_t = c_f.T
    for k in range(bits):
        rise_t[k * nstate : (k + 1) * nstate, :] = (c_t * far_t_ref[k : k + 1, :]).astype(BF16)
        lam = w_ref[:, low_bits + 1 + k : low_bits + 2 + k]
        rise[:, k * nstate : (k + 1) * nstate] = (c_f * lam).astype(BF16)
    pl.semaphore_wait(barrier, count - 1 + heads - 1)
    for q in range(chunks):
        cols = slice(q * WIDTH, (q + 1) * WIDTH)
        s_buf[q] = mm(b_t, x_ref[:, cols])
        x0_copy(q).start()
    for q in range(chunks):
        cols = slice(q * WIDTH, (q + 1) * WIDTH)
        g_buf[:, q] = mm(rise_t[...], d_ref[:, cols]).reshape(bits, nstate, WIDTH)
        if bits > 1:

            @pl.when(late[bits - 1])
            def _():
                back_copy(bits - 1, q).start()

    for k in reversed(range(1, bits - 1)):
        for q in range(chunks):

            @pl.when(late[k])
            def _():
                back_copy(k, q).start()

    def tile(i, j, diagonal):
        rows = pl.ds(i * TILE, TILE)
        cols = pl.ds(pl.multiple_of(j * TILE, TILE), TILE)
        w_rows = w_ref[rows, :]
        if diagonal:
            row = lax.broadcasted_iota(jnp.int32, (TILE, TILE), 0)
            at = lax.broadcasted_iota(jnp.int32, (TILE, TILE), 1)
            level = bit_count(row ^ at, tile_bits)
            weight = jnp.zeros((TILE, TILE), F32)
            for n in range(tile_bits + 1):
                weight = jnp.where(level == n, w_rows[:, n : n + 1], weight)
            weight = jnp.where(at <= row, weight, 0.0)
        else:
            far = i ^ j
            level = tile_bits
            for n in range(blocks.bit_length() - 1):
                level = level + (far >= 1 << n).astype(jnp.int32)
            lane = lax.broadcasted_iota(jnp.int32, w_rows.shape, 1)
            weight = jnp.sum(jnp.where(lane == level, w_rows, 0.0), axis=1, keepdims=True)
        x_j, d_i, b_j, c_i = x_ref[cols, :], d_ref[rows, :], b_ref[cols, :], c_ref[rows, :]
        mix = (mm_nt(c_i, b_j) * weight).astype(BF16)
        d_mix = (mm_nt(d_i, x_j) * weight).astype(BF16)
        y_t, dx_t = mm(mix, x_j), mm_tn(mix, d_i)
        dc_t, db_t = mm(d_mix, b_j), mm_tn(d_mix, c_i)
        if diagonal:
            y_acc[rows, :] = y_t
            dx_acc[cols, :] = dx_t
            grads[1, rows, :] = dc_t
            grads[0, cols, :] = db_t
        else:
            y_acc[rows, :] += y_t
            dx_acc[cols, :] += dx_t
            grads[1, rows, :] += dc_t
            grads[0, cols, :] += db_t

    def near(i):
        tile(i, i, True)
        if i:

            def step(j, none):
                tile(i, j, False)
                return none

            lax.fori_loop(0, i, step, 0)

    def pass_up(q):
        x0_copy(q).wait_recv()
        for k in levels:

            @pl.when(top[k])
            def _():
                group = s_buf[q] + rx0[q]
                for j in range(1, k):
                    up_copy(j, 0, q).wait_recv()
                    group = group + rc[j - 1, q]
                up[q] = group
                for step in range(1 << (k - 1)):
                    up_copy(k, step, q).start()

    def pass_down(q):
        if bits > 1:

            @pl.when(last)
            def _():
                tot[q] = jnp.zeros_like(tot[q])
        else:
            tot[q] = jnp.zeros_like(tot[q])

        for k in levels:

            @pl.when(top[k])
            def _():
                for step in range(1 << (k - 1)):
                    rb_wait(step, q)
                got = rb[0, q]
                for step in range(1, 1 << (k - 1)):
                    got = got + rb[step, q]
                tot[q] = got
                for j in range(1, k):
                    g_buf[j, q] = g_buf[j, q] + got
                    back_copy(j, q).start()

        @pl.when(par == 1)
        def _():
            xb[q] = tot[q] + g_buf[0, q]

        @pl.when(par == 0)
        def _():
            xb[q] = tot[q]

        xb_copy(q).start()

    def far(q):
        cols = slice(q * WIDTH, (q + 1) * WIDTH)
        for k in range(bits):
            at = slice(k * nstate, (k + 1) * nstate)
            if k:

                @pl.when(late[k])
                def _():
                    up_copy(k, 0, q).wait_recv()

            @pl.when(is_set[k])
            def _():
                carry[at, :] = (rc[k - 1, q] if k else rx0[q]).astype(BF16)

            @pl.when(jnp.logical_not(is_set[k]))
            def _():
                carry[at, :] = jnp.zeros((nstate, WIDTH), BF16)

        y_ref[:, cols] = (y_acc[:, cols] + mm(rise[...], carry[...])).astype(BF16)
        for i in range(blocks):
            rows = slice(i * TILE, (i + 1) * TILE)
            terms = mm_nt(d_ref[rows, cols], carry[...])
            total = grads[1, rows, :]
            for k in range(bits):
                lam = w_ref[rows, low_bits + 1 + k : low_bits + 2 + k]
                total = total + terms[:, k * nstate : (k + 1) * nstate] * lam
            grads[1, rows, :] = total
        xb_copy(q).wait_recv()
        back = (tot[q] + rxb[q]).astype(BF16)
        dx_ref[:, cols] = (dx_acc[:, cols] + mm(b_ref[...], back)).astype(BF16)
        grads[0] = grads[0] + mm_nt(x_ref[:, cols], back)

    for n in range(max(chunks, blocks)):
        if n < chunks:
            pass_up(n)
        if n < blocks:
            near(n)
    for n in range(chunks + 1):
        if n < chunks:
            pass_down(n)
        if n:
            far(n - 1)

    rows = toks // heads
    now, waits = [], []
    pieces = heads
    for digit in range(head_bits):
        pieces //= 2
        mine = (head // (1 << digit)) % 2
        peer = head + (1 - 2 * mine) * (1 << digit)
        ssem, rsem = hd_sems[2 * digit], hd_sems[2 * digit + 1]

        def piece(array, g, which):
            if digit == 0:
                start = pl.multiple_of((2 * g + which) * rows, rows)
                return grads.at[array, pl.ds(start, rows)]
            return r_out[digit - 1].at[array, 2 * g + which]

        copies = {}
        for array in range(2):
            for g in range(pieces):
                copies[array, g] = remote(
                    piece(array, g, 1 - mine),
                    r_in[digit].at[array, g],
                    ssem.at[array, g],
                    rsem.at[array, g],
                    {"head": peer},
                )
                copies[array, g].start()
        for array in range(2):
            for g in range(pieces):
                copies[array, g].wait_recv()
                value = piece(array, g, mine)[...] + r_in[digit][array, g]
                if digit < head_bits - 1:
                    r_out[digit][array, g] = value
                else:
                    (db_ref, dc_ref)[array][...] = value
        waits += list(copies.values())
    if not head_bits:
        db_ref[...] = grads[0]
        dc_ref[...] = grads[1]

    for copy in waits:
        copy.wait_send()
    for q in range(chunks):
        x0_copy(q).wait_send()
        xb_copy(q).wait_send()
        for k in levels:

            @pl.when(top[k])
            def _():
                for step in range(1 << (k - 1)):
                    up_copy(k, step, q).wait_send()

            @pl.when(is_set[k])
            def _():
                back_copy(k, q).wait_send()


def local(x_in, b_in, c_in, d_out, table, level_index):
    toks, feats = x_in.shape
    nstate = b_in.shape[1]
    count, heads = lax.axis_size("ctx"), lax.axis_size("head")
    bits, head_bits = count.bit_length() - 1, heads.bit_length() - 1
    low_bits = toks.bit_length() - 1
    chunks = feats // WIDTH
    chooser = (
        level_index[:, None] == jnp.arange(table.shape[0], dtype=jnp.int32)[None, :]
    ).astype(F32)
    w_tok = jnp.dot(chooser, table, precision=lax.Precision.HIGHEST)
    far_t = w_tok[:, low_bits + 1 : low_bits + 1 + bits].T
    rows = toks // heads
    fan = 1 << max(bits - 2, 0)
    ups = max(bits - 1, 1)
    vmem = pl.BlockSpec(memory_space=pltpu.VMEM)
    dma = pltpu.SemaphoreType.DMA
    slab = (chunks, nstate, WIDTH)
    halves = [heads >> (n + 1) for n in range(head_bits)]
    return pl.pallas_call(
        functools.partial(kernel, count, heads),
        out_shape=(
            jax.ShapeDtypeStruct((toks, feats), BF16),
            jax.ShapeDtypeStruct((toks, feats), BF16),
            jax.ShapeDtypeStruct((rows, nstate), F32),
            jax.ShapeDtypeStruct((rows, nstate), F32),
        ),
        in_specs=[vmem] * 6,
        out_specs=(vmem,) * 4,
        scratch_shapes=[
            pltpu.VMEM((toks, feats), F32),
            pltpu.VMEM((toks, feats), F32),
            pltpu.VMEM((2, toks, nstate), F32),
            pltpu.VMEM((toks, bits * nstate), BF16),
            pltpu.VMEM((bits * nstate, toks), BF16),
            pltpu.VMEM((bits * nstate, WIDTH), BF16),
            pltpu.VMEM(slab, F32),
            pltpu.VMEM((bits,) + slab, F32),
            pltpu.VMEM(slab, F32),
            pltpu.VMEM(slab, F32),
            pltpu.VMEM((ups,) + slab, F32),
            pltpu.VMEM((fan,) + slab, F32),
            pltpu.VMEM(slab, F32),
            pltpu.VMEM(slab, F32),
            pltpu.VMEM(slab, F32),
        ]
        + [pltpu.VMEM((2, half, rows, nstate), F32) for half in halves]
        + [pltpu.VMEM((2, half, rows, nstate), F32) for half in halves[:-1]]
        + [
            dma((chunks,)),
            dma((chunks,)),
            dma((fan, chunks)),
            dma((ups, chunks)),
            dma((ups, chunks)),
            dma((fan, chunks)),
            dma((chunks,)),
            dma((chunks,)),
        ]
        + [dma((2, half)) for half in halves for _ in range(2)],
        compiler_params=pltpu.CompilerParams(
            collective_id=0, has_side_effects=True, vmem_limit_bytes=60 * 1024 * 1024
        ),
    )(x_in, b_in, c_in, d_out, w_tok, far_t)


def solution(mesh):
    return jax.shard_map(
        local,
        mesh=mesh,
        in_specs=(
            P("ctx", "head"),
            P("ctx", None),
            P("ctx", None),
            P("ctx", "head"),
            P(),
            P("ctx"),
        ),
        out_specs=(
            P("ctx", "head"),
            P("ctx", "head"),
            P(("ctx", "head"), None),
            P(("ctx", "head"), None),
        ),
        check_vma=False,
    )
```

time: 198 us -> 68.5 us (0.35)
  waiting for transfers between devices: 103 us -> 0 us
  Pallas kernels: 0 us -> 57.7 us
  matrix products: 46.6 us -> 1.16 us
  between operations: 14.4 us -> 0.67 us
  other arithmetic: 13.3 us -> 0 us
  starting transfers between devices: 13.3 us -> 0 us
    ppermute x6 -> x0, waiting for transfers between devices: 87.9 us -> none  [from_partner(): return lax.ppermute(block, axis, route)]
    pallas_call x0 -> x1, Pallas kernels: none -> 57.7 us  [local(): pl.pallas_call(functools.partial(kernel, count, heads), out_shape=(jax.Sh...]
    dot_general x20 -> x1, matrix products: 46.6 us -> 1.16 us  [local(): w_tok = jnp.dot(chooser, table, precision=lax.Precision.HIGHEST)]
    reduce_scatter x2 -> x0, waiting for transfers between devices: 14.8 us -> none  [the longest x1 14.7 us: local(): lax.psum_scatter(grad_b, 'head', scatter_dimension=0, tiled=True)]
    ppermute x6 -> x0, starting transfers between devices: 13.2 us -> none  [from_partner(): return lax.ppermute(block, axis, route)]
    add x5 -> x0, other arithmetic: 4.22 us -> none  [the longest x1 2.07 us: local(): jnp.concatenate(c_parts, axis=0)]
    unnamed x52 -> x12, local copies, waits for them, and re-layouts: 2.63 us -> 6.56 us
    reshape x1 -> x0, local copies, waits for them, and re-layouts: 3.07 us -> none  [local(): jnp.dot(d_out, carry.T, preferred_element_type=jnp.float32)]
  transfers between devices with their start and end apart: 8 -> 0, of which waited for: 7 -> 0; matrix products, arithmetic and copies ran while one was open for 24% -> 0% of each run, Pallas kernels for 0% -> 0%
where the time goes in v1:
time: 68.5 us; the launch traced here: 67.7 us
  Pallas kernels  57.7 us (84%)
  local copies, waits for them, and re-layouts  8.19 us (12%)
  matrix products  1.16 us (2%)
    pallas_call x1, Pallas kernels, local(): pl.pallas_call(functools.partial(kernel, count, heads), out_shape=(jax.Sh...  57.7 us
    unnamed x12, local copies, waits for them, and re-layouts  6.56 us

profile of v1, /device:TPU:0, one launch (start us, length us, event | category | flops | bytes accessed | tf_op | source)
XLA Modules:
  0.0 67.7 jit_solution(5020711664335381747)
XLA Ops:
  0.6 0.0 copy-start
  0.6 0.7 %copy-done = f32[16,18]{1,0:T(8,128)S(1)} copy-done((f32[16,18]{1,0:T(8,128)S(1)}, f32[16,18]{1,0:T(8,128)}, u32[]{:S(2)}) %copy-start) | copy-done | bytes 1176
  1.3 1.2 %fusion = f32[1024,18]{0,1:T(8,128)S(1)} fusion(f32[16,18]{1,0:T(8,128)S(1)} %copy-done, s32[1024]{0:T(1024)} %param.11), kind=kOutput, calls=%fused_computation.1 | convolution fusion | flops 3555328 | bytes 78976 | tf_op jit(solution)/shard_map/dot_general | solution.py:368
  2.5 0.6 slice_bitcast_fusion.far_t_ref
  3.1 1.0 %copy.10.w_ref = f32[1024,18]{1,0:T(8,128)} copy(f32[1024,18]{0,1:T(8,128)S(1)} %fusion) | data formatting | bytes 147456 | tf_op jit(solution)/shard_map/dot_general | solution.py:368
  4.1 57.7 %shard_map.93 = (bf16[1024,1024]{1,0:T(8,128)(2,1)}, bf16[1024,1024]{1,0:T(8,128)(2,1)}, f32[256,128]{1,0:T(8,128)}, f32[256,128]{1,0:T(8,128)}) custom-call(bf16[1024,1024]{1,0:T(8,128)(2,1)} %x_ref.1, bf16[1024,128]{1,0:T(8,128)(2,1)} %b_ref.1, bf16[1024,128]{1,0:T(8,128)(2,1)} %c_ref.1, bf16[1024,1024]{1,0:T(8,128)(2,1)} %d_ref.1, ...), custom_call_target="tpu_custom_call" | custom-call | tf_op jit(solution)/shard_map/pallas_call | solution.py:377
  61.8 0.0 copy-start.1
  61.8 3.2 %copy.15 = bf16[1024,1024]{1,0:T(8,128)(2,1)} copy(bf16[1024,1024]{1,0:T(8,128)(2,1)} %get-tuple-element.8) | data formatting | bytes 4194304
  65.1 0.0 copy-done.1
  65.1 0.0 copy-start.3
  65.1 0.0 copy-start.2
  65.1 1.3 %copy.16 = bf16[1024,1024]{1,0:T(8,128)(2,1)} copy(bf16[1024,1024]{1,0:T(8,128)(2,1)S(1)} %copy-done.1) | data formatting | bytes 4194304
  66.4 0.0 copy-done.3
  66.4 0.7 copy.17
  67.1 0.0 copy-done.2
  67.1 0.7 copy.18
Async XLA Ops:
  0.6 0.7 %copy-start = (f32[16,18]{1,0:T(8,128)S(1)}, f32[16,18]{1,0:T(8,128)}, u32[]{:S(2)}) copy-start(f32[16,18]{1,0:T(8,128)} %param.10) | copy-start | bytes 3460
  61.8 3.2 %copy-start.1 = (bf16[1024,1024]{1,0:T(8,128)(2,1)S(1)}, bf16[1024,1024]{1,0:T(8,128)(2,1)}, u32[]{:S(2)}) copy-start(bf16[1024,1024]{1,0:T(8,128)(2,1)} %get-tuple-element.9) | copy-start | bytes 6291460
  65.1 1.3 %copy-start.3 = (f32[256,128]{1,0:T(8,128)S(1)}, f32[256,128]{1,0:T(8,128)}, u32[]{:S(2)}) copy-start(f32[256,128]{1,0:T(8,128)} %get-tuple-element.10) | copy-start | bytes 393220
  65.1 2.0 %copy-start.2 = (f32[256,128]{1,0:T(8,128)S(1)}, f32[256,128]{1,0:T(8,128)}, u32[]{:S(2)}) copy-start(f32[256,128]{1,0:T(8,128)} %get-tuple-element.11) | copy-start | bytes 393220

commit v2 on v1

v2 whole, which is shorter than its diff:
```python
import functools

import jax
import jax.numpy as jnp
from jax import lax
from jax.experimental import pallas as pl
from jax.experimental.pallas import tpu as pltpu
from jax.sharding import PartitionSpec as P

F32 = jnp.float32
BF16 = jnp.bfloat16
MESH = pl.DeviceIdType.MESH
TILE = 256
WIDTH = 256


def mm(a, b):
    return jnp.dot(a, b, preferred_element_type=F32)


def mm_tn(a, b):
    return lax.dot_general(a, b, (((0,), (0,)), ((), ())), preferred_element_type=F32)


def mm_nt(a, b):
    return lax.dot_general(a, b, (((1,), (1,)), ((), ())), preferred_element_type=F32)


def bit_count(values, bits):
    counted = jnp.zeros(values.shape, jnp.int32)
    for digit_no in range(bits):
        counted = counted + (values >= 1 << digit_no).astype(jnp.int32)
    return counted


def kernel(
    count,
    heads,
    x_hbm,
    b_ref,
    c_ref,
    d_hbm,
    table_ref,
    index_ref,
    y_ref,
    dx_ref,
    db_ref,
    dc_ref,
    x_ref,
    d_ref,
    w_ref,
    y_acc,
    dx_acc,
    grads,
    rise,
    rise_t,
    carry,
    s_buf,
    g_buf,
    rx0,
    up,
    rc,
    rb,
    tot,
    xb,
    rxb,
    *rest,
):
    bits = count.bit_length() - 1
    head_bits = heads.bit_length() - 1
    r_in = rest[:head_bits]
    r_out = rest[head_bits : 2 * head_bits - 1]
    sems = rest[2 * head_bits - 1 :]
    in_sem, x0_s, x0_r, up_s, fw_s, rc_r, bk_s, rb_r, xb_s, xb_r = sems[:10]
    hd_sems = sems[10:]
    toks, feats = x_ref.shape
    nstate = b_ref.shape[1]
    chunks = feats // WIDTH
    blocks = toks // TILE
    tile_bits = TILE.bit_length() - 1
    low_bits = toks.bit_length() - 1
    me = lax.axis_index("ctx")
    head = lax.axis_index("head")
    par = me % 2
    col = me // 2
    levels = range(1, bits)
    columns = count // 2
    is_set = {k: (me // (1 << k)) % 2 == 1 for k in range(bits)}
    low_top = {k: col % (1 << k) == (1 << (k - 1)) - 1 for k in levels}
    up_top = {k: col % (1 << k) == (1 << k) - 1 for k in levels}
    relay = {k: is_set[k] & jnp.logical_not(up_top[k]) for k in levels}
    last = col == columns - 1
    ready = {k: up_top[k] & last for k in levels}
    early = {k: up_top[k] & jnp.logical_not(last) for k in levels}
    late = {k: up_top[k] & last for k in levels}

    def fill(hbm, vmem, n, q):
        cols = pl.ds(q * WIDTH, WIDTH)
        return pltpu.make_async_copy(hbm.at[:, cols], vmem.at[:, cols], in_sem.at[n, q])

    for q in range(chunks):
        fill(x_hbm, x_ref, 0, q).start()
    for q in range(chunks):
        fill(d_hbm, d_ref, 1, q).start()

    partner = me + 1 - 2 * par
    barrier = pltpu.get_barrier_semaphore()
    pl.semaphore_signal(barrier, inc=1, device_id={"ctx": partner}, device_id_type=MESH)
    for digit in range(head_bits):
        flip = 1 - 2 * ((head // (1 << digit)) % 2)
        pl.semaphore_signal(
            barrier, inc=1, device_id={"head": head + flip * (1 << digit)}, device_id_type=MESH
        )

    @pl.when(col > 0)
    def _():
        pl.semaphore_signal(barrier, inc=1, device_id={"ctx": me - 2}, device_id_type=MESH)

    @pl.when(col < columns - 1)
    def _():
        pl.semaphore_signal(barrier, inc=1, device_id={"ctx": me + 2}, device_id_type=MESH)

    def remote(src, dst, ssem, rsem, device):
        return pltpu.make_async_remote_copy(
            src_ref=src,
            dst_ref=dst,
            send_sem=ssem,
            recv_sem=rsem,
            device_id=device,
            device_id_type=MESH,
        )

    def x0_copy(q):
        return remote(s_buf.at[q], rx0.at[q], x0_s.at[q], x0_r.at[q], {"ctx": partner})

    def up_copy(k, q):
        return remote(
            up.at[q], rc.at[k - 1, q], up_s.at[q], rc_r.at[k - 1, q], {"ctx": me + 2}
        )

    def forward_copy(k, q):
        return remote(
            rc.at[k - 1, q],
            rc.at[k - 1, q],
            fw_s.at[k - 1, q],
            rc_r.at[k - 1, q],
            {"ctx": me + 2},
        )

    def back_copy(k, q):
        return remote(
            g_buf.at[k, q],
            rb.at[k - 1, q],
            bk_s.at[k - 1, q],
            rb_r.at[k - 1, q],
            {"ctx": me - 2},
        )

    def xb_copy(q):
        return remote(xb.at[q], rxb.at[q], xb_s.at[q], xb_r.at[q], {"ctx": partner})

    hot = (
        lax.broadcasted_iota(jnp.int32, (table_ref.shape[0], toks), 0) == index_ref[...]
    ).astype(F32)
    w_t = lax.dot_general(
        table_ref[...],
        hot,
        (((0,), (0,)), ((), ())),
        preferred_element_type=F32,
        precision=lax.Precision.HIGHEST,
    )
    w_ref[...] = w_t.T
    b_t = b_ref[...].astype(F32).T.astype(BF16)
    c_f = c_ref[...].astype(F32)
    c_t = c_f.T
    for k in range(bits):
        lam_t = w_t[low_bits + 1 + k : low_bits + 2 + k, :]
        rise_t[k * nstate : (k + 1) * nstate, :] = (c_t * lam_t).astype(BF16)

    ends = (col > 0).astype(jnp.int32) + (col < columns - 1).astype(jnp.int32)
    pl.semaphore_wait(barrier, 1 + head_bits + ends)

    for q in range(chunks):
        cols = slice(q * WIDTH, (q + 1) * WIDTH)
        fill(x_hbm, x_ref, 0, q).wait()
        s_buf[q] = mm(b_t, x_ref[:, cols])
        x0_copy(q).start()
    for q in range(chunks):
        cols = slice(q * WIDTH, (q + 1) * WIDTH)
        fill(d_hbm, d_ref, 1, q).wait()
        g_buf[:, q] = mm(rise_t[...], d_ref[:, cols]).reshape(bits, nstate, WIDTH)
        if bits > 1:

            @pl.when(ready[bits - 1])
            def _():
                back_copy(bits - 1, q).start()

    for k in reversed(range(1, bits - 1)):
        for q in range(chunks):

            @pl.when(ready[k])
            def _():
                back_copy(k, q).start()

    def tile(i, j):
        rows = slice(i * TILE, (i + 1) * TILE)
        cols = slice(j * TILE, (j + 1) * TILE)
        w_rows = w_ref[rows, :]
        if i == j:
            row = lax.broadcasted_iota(jnp.int32, (TILE, TILE), 0)
            at = lax.broadcasted_iota(jnp.int32, (TILE, TILE), 1)
            level = bit_count(row ^ at, tile_bits)
            weight = jnp.zeros((TILE, TILE), F32)
            for n in range(tile_bits + 1):
                weight = jnp.where(level == n, w_rows[:, n : n + 1], weight)
            weight = jnp.where(at <= row, weight, 0.0)
        else:
            level = tile_bits + (i ^ j).bit_length()
            weight = w_rows[:, level : level + 1]
        x_j, d_i, b_j, c_i = x_ref[cols, :], d_ref[rows, :], b_ref[cols, :], c_ref[rows, :]
        mix = (mm_nt(c_i, b_j) * weight).astype(BF16)
        d_mix = (mm_nt(d_i, x_j) * weight).astype(BF16)
        y_t, dx_t = mm(mix, x_j), mm_tn(mix, d_i)
        dc_t, db_t = mm(d_mix, b_j), mm_tn(d_mix, c_i)
        if i == j:
            y_acc[rows, :] = y_t
            dx_acc[cols, :] = dx_t
            grads[1, rows, :] = dc_t
            grads[0, cols, :] = db_t
        else:
            y_acc[rows, :] += y_t
            dx_acc[cols, :] += dx_t
            grads[1, rows, :] += dc_t
            grads[0, cols, :] += db_t

    def pass_up(q):
        x0_copy(q).wait_recv()
        for k in levels:

            @pl.when(low_top[k])
            def _():
                group = s_buf[q] + rx0[q]
                for j in range(1, k):
                    up_copy(j, q).wait_recv()
                    group = group + rc[j - 1, q]
                up[q] = group
                up_copy(k, q).start()

    def relay_up(q):
        for k in levels:

            @pl.when(relay[k])
            def _():
                up_copy(k, q).wait_recv()
                forward_copy(k, q).start()

    def relay_down(q):
        for k in reversed(levels):

            @pl.when(relay[k])
            def _():
                back_copy(k, q).wait_recv()
                g_buf[k, q] = g_buf[k, q] + rb[k - 1, q]
                back_copy(k, q).start()

    def pass_down(q):
        @pl.when(last)
        def _():
            tot[q] = jnp.zeros_like(tot[q])

        for k in levels:

            @pl.when(low_top[k])
            def _():
                back_copy(k, q).wait_recv()
                got = rb[k - 1, q]
                tot[q] = got
                for j in range(1, k):
                    g_buf[j, q] = g_buf[j, q] + got
                    back_copy(j, q).start()

        @pl.when(par == 1)
        def _():
            xb[q] = tot[q] + g_buf[0, q]

        @pl.when(par == 0)
        def _():
            xb[q] = tot[q]

        xb_copy(q).start()

    def far_up(q):
        cols = slice(q * WIDTH, (q + 1) * WIDTH)
        for k in range(bits):
            at = slice(k * nstate, (k + 1) * nstate)
            if k:

                @pl.when(late[k])
                def _():
                    up_copy(k, q).wait_recv()

            @pl.when(is_set[k])
            def _():
                carry[at, :] = (rc[k - 1, q] if k else rx0[q]).astype(BF16)

            @pl.when(jnp.logical_not(is_set[k]))
            def _():
                carry[at, :] = jnp.zeros((nstate, WIDTH), BF16)

        y_ref[:, cols] = (y_acc[:, cols] + mm(rise[...], carry[...])).astype(BF16)
        for i in range(blocks):
            rows = slice(i * TILE, (i + 1) * TILE)
            terms = mm_nt(d_ref[rows, cols], carry[...])
            total = grads[1, rows, :]
            for k in range(bits):
                lam = w_ref[rows, low_bits + 1 + k : low_bits + 2 + k]
                total = total + terms[:, k * nstate : (k + 1) * nstate] * lam
            grads[1, rows, :] = total

    def far_down(q):
        cols = slice(q * WIDTH, (q + 1) * WIDTH)
        xb_copy(q).wait_recv()
        back = (tot[q] + rxb[q]).astype(BF16)
        dx_ref[:, cols] = (dx_acc[:, cols] + mm(b_ref[...], back)).astype(BF16)
        grads[0] = grads[0] + mm_nt(x_ref[:, cols], back)

    part = toks // heads
    waits = []

    def piece(array, digit, g, which):
        if digit == 0:
            start = pl.multiple_of((2 * g + which) * part, part)
            return grads.at[array, pl.ds(start, part)]
        return r_out[digit - 1].at[array, 2 * g + which]

    def halve_start(array, digit):
        mine = (head // (1 << digit)) % 2
        peer = head + (1 - 2 * mine) * (1 << digit)
        copies = []
        for g in range(heads >> (digit + 1)):
            copies.append(
                remote(
                    piece(array, digit, g, 1 - mine),
                    r_in[digit].at[array, g],
                    hd_sems[2 * digit].at[array, g],
                    hd_sems[2 * digit + 1].at[array, g],
                    {"head": peer},
                )
            )
            copies[-1].start()
        waits.extend(copies)
        return copies

    def halve_end(array, digit, copies):
        mine = (head // (1 << digit)) % 2
        for g, copy in enumerate(copies):
            copy.wait_recv()
            value = piece(array, digit, g, mine)[...] + r_in[digit][array, g]
            if digit < head_bits - 1:
                r_out[digit][array, g] = value
            else:
                (db_ref, dc_ref)[array][...] = value

    tiles = [(i, i) for i in range(blocks)]
    tiles += [(i, j) for i in range(blocks) for j in range(i)]

    def near(amount):
        for _ in range(min(amount, len(tiles))):
            tile(*tiles.pop(0))

    def pass_down_if(condition, q):
        @pl.when(condition)
        def _():
            pass_down(q)

    slow = low_top[1] if bits > 1 else col < 0
    quick = jnp.logical_not(slow)
    for n in range(chunks + 2):
        if n < chunks:
            pass_up(n)
        if 0 < n <= chunks:
            relay_down(n - 1)
        if n > 1:
            pass_down_if(quick, n - 2)
        near(1)
    for k in range(bits):
        lam = w_ref[:, low_bits + 1 + k : low_bits + 2 + k]
        rise[:, k * nstate : (k + 1) * nstate] = (c_f * lam).astype(BF16)
    for n in range(chunks + 1):
        if n < chunks:
            relay_up(n)
        near(1)
        if n:
            pass_down_if(slow, n - 1)
    near(len(tiles))
    for n in range(chunks):
        far_up(n)
    jobs = halve_start(1, 0) if head_bits else []
    for n in range(chunks):
        far_down(n)
    jobs_b = halve_start(0, 0) if head_bits else []
    for digit in range(head_bits):
        halve_end(1, digit, jobs)
        if digit < head_bits - 1:
            jobs = halve_start(1, digit + 1)
        halve_end(0, digit, jobs_b)
        if digit < head_bits - 1:
            jobs_b = halve_start(0, digit + 1)
    if not head_bits:
        db_ref[...] = grads[0]
        dc_ref[...] = grads[1]

    for copy in waits:
        copy.wait_send()
    for q in range(chunks):
        x0_copy(q).wait_send()
        xb_copy(q).wait_send()
        for k in levels:

            @pl.when(low_top[k])
            def _():
                up_copy(k, q).wait_send()

            @pl.when(relay[k])
            def _():
                forward_copy(k, q).wait_send()

            @pl.when(is_set[k])
            def _():
                back_copy(k, q).wait_send()


def local(x_in, b_in, c_in, d_out, table, level_index):
    toks, feats = x_in.shape
    nstate = b_in.shape[1]
    count, heads = lax.axis_size("ctx"), lax.axis_size("head")
    bits, head_bits = count.bit_length() - 1, heads.bit_length() - 1
    chunks = feats // WIDTH
    table = jnp.pad(table, ((0, 0), (0, nstate - table.shape[1])))
    index = level_index.reshape(1, toks)
    rows = toks // heads
    ups = max(bits - 1, 1)
    vmem = pl.BlockSpec(memory_space=pltpu.VMEM)
    hbm = pl.BlockSpec(memory_space=pl.ANY)
    dma = pltpu.SemaphoreType.DMA
    slab = (chunks, nstate, WIDTH)
    halves = [heads >> (n + 1) for n in range(head_bits)]
    return pl.pallas_call(
        functools.partial(kernel, count, heads),
        out_shape=(
            pltpu.VMEM((toks, feats), BF16),
            pltpu.VMEM((toks, feats), BF16),
            pltpu.VMEM((rows, nstate), F32),
            pltpu.VMEM((rows, nstate), F32),
        ),
        in_specs=[hbm, vmem, vmem, hbm, vmem, vmem],
        out_specs=(vmem,) * 4,
        scratch_shapes=[
            pltpu.VMEM((toks, feats), BF16),
            pltpu.VMEM((toks, feats), BF16),
            pltpu.VMEM((toks, nstate), F32),
            pltpu.VMEM((toks, feats), F32),
            pltpu.VMEM((toks, feats), F32),
            pltpu.VMEM((2, toks, nstate), F32),
            pltpu.VMEM((toks, bits * nstate), BF16),
            pltpu.VMEM((bits * nstate, toks), BF16),
            pltpu.VMEM((bits * nstate, WIDTH), BF16),
            pltpu.VMEM(slab, F32),
            pltpu.VMEM((bits,) + slab, F32),
            pltpu.VMEM(slab, F32),
            pltpu.VMEM(slab, F32),
            pltpu.VMEM((ups,) + slab, F32),
            pltpu.VMEM((ups,) + slab, F32),
            pltpu.VMEM(slab, F32),
            pltpu.VMEM(slab, F32),
            pltpu.VMEM(slab, F32),
        ]
        + [pltpu.VMEM((2, half, rows, nstate), F32) for half in halves]
        + [pltpu.VMEM((2, half, rows, nstate), F32) for half in halves[:-1]]
        + [
            dma((2, chunks)),
            dma((chunks,)),
            dma((chunks,)),
            dma((chunks,)),
            dma((ups, chunks)),
            dma((ups, chunks)),
            dma((ups, chunks)),
            dma((ups, chunks)),
            dma((chunks,)),
            dma((chunks,)),
        ]
        + [dma((2, half)) for half in halves for _ in range(2)],
        compiler_params=pltpu.CompilerParams(
            collective_id=0, has_side_effects=True, vmem_limit_bytes=48 * 1024 * 1024
        ),
    )(x_in, b_in, c_in, d_out, table, index)


def solution(mesh):
    return jax.shard_map(
        local,
        mesh=mesh,
        in_specs=(
            P("ctx", "head"),
            P("ctx", None),
            P("ctx", None),
            P("ctx", "head"),
            P(),
            P("ctx"),
        ),
        out_specs=(
            P("ctx", "head"),
            P("ctx", "head"),
            P(("ctx", "head"), None),
            P(("ctx", "head"), None),
        ),
        check_vma=False,
    )
```

time: 68.5 us -> 54.1 us (0.79)
  Pallas kernels: 57.7 us -> 45.9 us
  matrix products: 1.16 us -> 0 us
  local copies, waits for them, and re-layouts: 8.19 us -> 7.24 us
    pallas_call x1, Pallas kernels: 57.7 us -> 45.9 us  [local(): pl.pallas_call(functools.partial(kernel, count, heads), out_shape=(pltpu....]
    dot_general x1 -> x0, matrix products: 1.16 us -> none  [local(): w_tok = jnp.dot(chooser, table, precision=lax.Precision.HIGHEST)]
    dot_general x1 -> x0, local copies, waits for them, and re-layouts: 1.02 us -> none  [local(): w_tok = jnp.dot(chooser, table, precision=lax.Precision.HIGHEST)]
    pad x0 -> x1, local copies, waits for them, and re-layouts: none -> 0.7 us  [local(): table = jnp.pad(table, ((0, 0), (0, nstate - table.shape[1])))]
    unnamed x12 -> x10, local copies, waits for them, and re-layouts: 6.56 us -> 6.53 us
where the time goes in v2:
time: 54.1 us; the launch traced here: 53.8 us
  Pallas kernels  45.9 us (85%)
  local copies, waits for them, and re-layouts  7.24 us (13%)
  between operations  0.64 us (1%)
    pallas_call x1, Pallas kernels, local(): pl.pallas_call(functools.partial(kernel, count, heads), out_shape=(pltpu....  45.9 us
    unnamed x10, local copies, waits for them, and re-layouts  6.53 us

profile of v2, /device:TPU:0, one launch (start us, length us, event | category | flops | bytes accessed | tf_op | source)
XLA Modules:
  0.0 53.8 jit_solution(5828501184537755350)
XLA Ops:
  0.6 0.7 %pad.4.table_ref = f32[16,128]{1,0:T(8,128)S(1)} pad(f32[16,18]{1,0:T(8,128)} %param.10, f32[]{:T(128)} %constant.2.clone.1), padding=0_0x0_110 | pad | bytes 9348 | tf_op jit(solution)/shard_map/jit(_pad)/pad | solution.py:439
  1.3 0.0 copy-start
  1.3 0.9 %copy-done = bf16[1024,128]{1,0:T(8,128)(2,1)S(1)} copy-done((bf16[1024,128]{1,0:T(8,128)(2,1)S(1)}, bf16[1024,128]{1,0:T(8,128)(2,1)}, u32[]{:S(2)}) %copy-start) | copy-done | bytes 262168
  2.3 0.0 copy-start.1
  2.3 0.9 %copy-done.1 = bf16[1024,128]{1,0:T(8,128)(2,1)S(1)} copy-done((bf16[1024,128]{1,0:T(8,128)(2,1)S(1)}, bf16[1024,128]{1,0:T(8,128)(2,1)}, u32[]{:S(2)}) %copy-start.1) | copy-done | bytes 262168
  3.2 0.0 copy-start.2
  3.2 0.7 %copy-done.2 = s32[1024]{0:T(1024)S(1)} copy-done((s32[1024]{0:T(1024)S(1)}, s32[1024]{0:T(1024)}, u32[]{:S(2)}) %copy-start.2) | copy-done | bytes 4120
  3.9 45.9 %shard_map.93 = (bf16[1024,1024]{1,0:T(8,128)(2,1)S(1)}, bf16[1024,1024]{1,0:T(8,128)(2,1)S(1)}, f32[256,128]{1,0:T(8,128)S(1)}, f32[256,128]{1,0:T(8,128)S(1)}) custom-call(bf16[1024,1024]{1,0:T(8,128)(2,1)} %x_hbm.1, bf16[1024,128]{1,0:T(8,128)(2,1)S(1)} %copy-done, bf16[1024,128]{1,0:T(8,128)(2,1)S(1)} %copy-done.1, bf16[1024,1024]{1,0:T(8,128)(2,1)} %d_hbm.1, ...), custom_call_target="tpu_custom_call" | custom-call | tf_op jit(solution)/shard_map/pallas_call | solution.py:448
  49.9 1.3 %copy.14 = bf16[1024,1024]{1,0:T(8,128)(2,1)} copy(bf16[1024,1024]{1,0:T(8,128)(2,1)S(1)} %get-tuple-element.4) | data formatting | bytes 4194304
  51.2 0.7 %copy.16 = f32[256,128]{1,0:T(8,128)} copy(f32[256,128]{1,0:T(8,128)S(1)} %get-tuple-element.6) | data formatting | bytes 262144
  51.8 0.7 %copy.17 = f32[256,128]{1,0:T(8,128)} copy(f32[256,128]{1,0:T(8,128)S(1)} %get-tuple-element.7) | data formatting | bytes 262144
  52.5 1.3 %copy.15 = bf16[1024,1024]{1,0:T(8,128)(2,1)} copy(bf16[1024,1024]{1,0:T(8,128)(2,1)S(1)} %get-tuple-element.5) | data formatting | bytes 4194304
Async XLA Ops:
  1.3 0.9 %copy-start = (bf16[1024,128]{1,0:T(8,128)(2,1)S(1)}, bf16[1024,128]{1,0:T(8,128)(2,1)}, u32[]{:S(2)}) copy-start(bf16[1024,128]{1,0:T(8,128)(2,1)} %b_ref.1) | copy-start | bytes 786436
  2.3 0.9 %copy-start.1 = (bf16[1024,128]{1,0:T(8,128)(2,1)S(1)}, bf16[1024,128]{1,0:T(8,128)(2,1)}, u32[]{:S(2)}) copy-start(bf16[1024,128]{1,0:T(8,128)(2,1)} %c_ref.1) | copy-start | bytes 786436
  3.2 0.7 %copy-start.2 = (s32[1024]{0:T(1024)S(1)}, s32[1024]{0:T(1024)}, u32[]{:S(2)}) copy-start(s32[1024]{0:T(1024)} %param.11) | copy-start | bytes 12292

commit v3 on v2

--- a/solution.py
+++ b/solution.py
@@ -12,6 +12,8 @@
 MESH = pl.DeviceIdType.MESH
 TILE = 256
 WIDTH = 256
+VMEM_BYTES = 67043328
+SPARE = 16384
 
 
 def mm(a, b):
@@ -37,17 +39,22 @@
     count,
     heads,
     x_hbm,
-    b_ref,
-    c_ref,
+    b_hbm,
+    c_hbm,
     d_hbm,
-    table_ref,
-    index_ref,
+    table_hbm,
+    index_hbm,
     y_ref,
     dx_ref,
     db_ref,
     dc_ref,
     x_ref,
     d_ref,
+    b_ref,
+    c_ref,
+    table_ref,
+    index_ref,
+    wide_table,
     w_ref,
     y_acc,
     dx_acc,
@@ -71,8 +78,8 @@
     r_in = rest[:head_bits]
     r_out = rest[head_bits : 2 * head_bits - 1]
     sems = rest[2 * head_bits - 1 :]
-    in_sem, x0_s, x0_r, up_s, fw_s, rc_r, bk_s, rb_r, xb_s, xb_r = sems[:10]
-    hd_sems = sems[10:]
+    small_sem, in_sem, x0_s, x0_r, up_s, fw_s, rc_r, bk_s, rb_r, xb_s, xb_r = sems[:11]
+    hd_sems = sems[11:]
     toks, feats = x_ref.shape
     nstate = b_ref.shape[1]
     chunks = feats // WIDTH
@@ -98,8 +105,22 @@
         cols = pl.ds(q * WIDTH, WIDTH)
         return pltpu.make_async_copy(hbm.at[:, cols], vmem.at[:, cols], in_sem.at[n, q])
 
+    smalls = [
+        pltpu.make_async_copy(hbm, vmem, small_sem.at[n])
+        for n, (hbm, vmem) in enumerate(
+            (
+                (b_hbm, b_ref),
+                (c_hbm, c_ref),
+                (table_hbm, table_ref),
+                (index_hbm, index_ref),
+            )
+        )
+    ]
+    smalls[0].start()
     for q in range(chunks):
         fill(x_hbm, x_ref, 0, q).start()
+    for small in smalls[1:]:
+        small.start()
     for q in range(chunks):
         fill(d_hbm, d_ref, 1, q).start()
 
@@ -159,32 +180,38 @@
     def xb_copy(q):
         return remote(xb.at[q], rxb.at[q], xb_s.at[q], xb_r.at[q], {"ctx": partner})
 
+    smalls[0].wait()
+    b_t = b_ref[...].astype(F32).T.astype(BF16)
+    ends = (col > 0).astype(jnp.int32) + (col < columns - 1).astype(jnp.int32)
+    pl.semaphore_wait(barrier, 1 + head_bits + ends)
+
+    for q in range(chunks):
+        cols = slice(q * WIDTH, (q + 1) * WIDTH)
+        fill(x_hbm, x_ref, 0, q).wait()
+        s_buf[q] = mm(b_t, x_ref[:, cols])
+        x0_copy(q).start()
+
+    for small in smalls[1:]:
+        small.wait()
+    wide_table[...] = jnp.zeros_like(wide_table)
+    wide_table[:, : table_ref.shape[1]] = table_ref[...]
     hot = (
         lax.broadcasted_iota(jnp.int32, (table_ref.shape[0], toks), 0) == index_ref[...]
     ).astype(F32)
     w_t = lax.dot_general(
-        table_ref[...],
+        wide_table[...],
         hot,
         (((0,), (0,)), ((), ())),
         preferred_element_type=F32,
         precision=lax.Precision.HIGHEST,
     )
     w_ref[...] = w_t.T
-    b_t = b_ref[...].astype(F32).T.astype(BF16)
     c_f = c_ref[...].astype(F32)
     c_t = c_f.T
     for k in range(bits):
         lam_t = w_t[low_bits + 1 + k : low_bits + 2 + k, :]
         rise_t[k * nstate : (k + 1) * nstate, :] = (c_t * lam_t).astype(BF16)
 
-    ends = (col > 0).astype(jnp.int32) + (col < columns - 1).astype(jnp.int32)
-    pl.semaphore_wait(barrier, 1 + head_bits + ends)
-
-    for q in range(chunks):
-        cols = slice(q * WIDTH, (q + 1) * WIDTH)
-        fill(x_hbm, x_ref, 0, q).wait()
-        s_buf[q] = mm(b_t, x_ref[:, cols])
-        x0_copy(q).start()
     for q in range(chunks):
         cols = slice(q * WIDTH, (q + 1) * WIDTH)
         fill(d_hbm, d_ref, 1, q).wait()
@@ -375,37 +402,37 @@
 
     slow = low_top[1] if bits > 1 else col < 0
     quick = jnp.logical_not(slow)
-    for n in range(chunks + 2):
+    slots = chunks + 2
+    for n in range(slots):
         if n < chunks:
             pass_up(n)
         if 0 < n <= chunks:
             relay_down(n - 1)
         if n > 1:
             pass_down_if(quick, n - 2)
-        near(1)
+        near(pl.cdiv(len(tiles), slots - n))
     for k in range(bits):
         lam = w_ref[:, low_bits + 1 + k : low_bits + 2 + k]
         rise[:, k * nstate : (k + 1) * nstate] = (c_f * lam).astype(BF16)
     for n in range(chunks + 1):
         if n < chunks:
             relay_up(n)
-        near(1)
         if n:
             pass_down_if(slow, n - 1)
-    near(len(tiles))
-    for n in range(chunks):
-        far_up(n)
+        if n < chunks:
+            far_up(n)
     jobs = halve_start(1, 0) if head_bits else []
     for n in range(chunks):
         far_down(n)
-    jobs_b = halve_start(0, 0) if head_bits else []
+        if n == max(chunks // 2 - 1, 0) and head_bits:
+            halve_end(1, 0, jobs)
+            jobs = halve_start(1, 1) if head_bits > 1 else []
     for digit in range(head_bits):
-        halve_end(1, digit, jobs)
-        if digit < head_bits - 1:
-            jobs = halve_start(1, digit + 1)
+        jobs_b = halve_start(0, digit)
+        if digit:
+            halve_end(1, digit, jobs)
+            jobs = halve_start(1, digit + 1) if digit < head_bits - 1 else []
         halve_end(0, digit, jobs_b)
-        if digit < head_bits - 1:
-            jobs_b = halve_start(0, digit + 1)
     if not head_bits:
         db_ref[...] = grads[0]
         dc_ref[...] = grads[1]
@@ -430,22 +457,29 @@
                 back_copy(k, q).wait_send()
 
 
+def write_out(*refs):
+    copies = [pltpu.make_async_copy(refs[n], refs[n + 4], refs[8].at[n]) for n in range(4)]
+    for copy in copies:
+        copy.start()
+    for copy in copies:
+        copy.wait()
+
+
 def local(x_in, b_in, c_in, d_out, table, level_index):
     toks, feats = x_in.shape
     nstate = b_in.shape[1]
     count, heads = lax.axis_size("ctx"), lax.axis_size("head")
     bits, head_bits = count.bit_length() - 1, heads.bit_length() - 1
     chunks = feats // WIDTH
-    table = jnp.pad(table, ((0, 0), (0, nstate - table.shape[1])))
     index = level_index.reshape(1, toks)
     rows = toks // heads
     ups = max(bits - 1, 1)
     vmem = pl.BlockSpec(memory_space=pltpu.VMEM)
-    hbm = pl.BlockSpec(memory_space=pl.ANY)
+    hbm = pl.BlockSpec(memory_space=pltpu.HBM)
     dma = pltpu.SemaphoreType.DMA
     slab = (chunks, nstate, WIDTH)
     halves = [heads >> (n + 1) for n in range(head_bits)]
-    return pl.pallas_call(
+    results = pl.pallas_call(
         functools.partial(kernel, count, heads),
         out_shape=(
             pltpu.VMEM((toks, feats), BF16),
@@ -453,11 +487,16 @@
             pltpu.VMEM((rows, nstate), F32),
             pltpu.VMEM((rows, nstate), F32),
         ),
-        in_specs=[hbm, vmem, vmem, hbm, vmem, vmem],
+        in_specs=[hbm] * 6,
         out_specs=(vmem,) * 4,
         scratch_shapes=[
             pltpu.VMEM((toks, feats), BF16),
             pltpu.VMEM((toks, feats), BF16),
+            pltpu.VMEM((toks, nstate), BF16),
+            pltpu.VMEM((toks, nstate), BF16),
+            pltpu.VMEM(table.shape, F32),
+            pltpu.VMEM((1, toks), jnp.int32),
+            pltpu.VMEM((table.shape[0], nstate), F32),
             pltpu.VMEM((toks, nstate), F32),
             pltpu.VMEM((toks, feats), F32),
             pltpu.VMEM((toks, feats), F32),
@@ -478,6 +517,7 @@
         + [pltpu.VMEM((2, half, rows, nstate), F32) for half in halves]
         + [pltpu.VMEM((2, half, rows, nstate), F32) for half in halves[:-1]]
         + [
+            dma((4,)),
             dma((2, chunks)),
             dma((chunks,)),
             dma((chunks,)),
@@ -491,9 +531,17 @@
         ]
         + [dma((2, half)) for half in halves for _ in range(2)],
         compiler_params=pltpu.CompilerParams(
-            collective_id=0, has_side_effects=True, vmem_limit_bytes=48 * 1024 * 1024
+            collective_id=0, has_side_effects=True, vmem_limit_bytes=VMEM_BYTES - 4 * toks * feats - 8 * rows * nstate - SPARE
         ),
     )(x_in, b_in, c_in, d_out, table, index)
+    return pl.pallas_call(
+        write_out,
+        out_shape=tuple(jax.ShapeDtypeStruct(r.shape, r.dtype) for r in results),
+        in_specs=[vmem] * 4,
+        out_specs=(hbm,) * 4,
+        scratch_shapes=[dma((4,))],
+        compiler_params=pltpu.CompilerParams(vmem_limit_bytes=1024 * 1024),
+    )(*results)
 
 
 def solution(mesh):

time: 54.1 us -> 46.3 us (0.86)
  local copies, waits for them, and re-layouts: 7.24 us -> 0 us
  Pallas kernels: 45.9 us -> 45.2 us
    unnamed x10 -> x0, local copies, waits for them, and re-layouts: 6.53 us -> none
    pallas_call x1, Pallas kernels: 45.9 us -> 43.1 us  [local(): pl.pallas_call(functools.partial(kernel, count, heads), out_shape=(pltpu....]
    pallas_call x0 -> x1, Pallas kernels: none -> 2.11 us  [local(): pl.pallas_call(write_out, out_shape=tuple((jax.ShapeDtypeStruct(r.shape,...]
    pad x1 -> x0, local copies, waits for them, and re-layouts: 0.7 us -> none  [local(): table = jnp.pad(table, ((0, 0), (0, nstate - table.shape[1])))]
where the time goes in v3:
time: 46.3 us; the launch traced here: 46.1 us
  Pallas kernels  45.2 us (98%)
  between operations  0.8 us (2%)
    pallas_call x1, Pallas kernels, local(): pl.pallas_call(functools.partial(kernel, count, heads), out_shape=(pltpu....  43.1 us
    pallas_call x1, Pallas kernels, local(): pl.pallas_call(write_out, out_shape=tuple((jax.ShapeDtypeStruct(r.shape,...  2.11 us

profile of v3, /device:TPU:0, one launch (start us, length us, event | category | flops | bytes accessed | tf_op | source)
XLA Modules:
  0.0 46.1 jit_solution(1360510522022385426)
XLA Ops:
  0.6 43.1 %shard_map.93 = (bf16[1024,1024]{1,0:T(8,128)(2,1)S(1)}, bf16[1024,1024]{1,0:T(8,128)(2,1)S(1)}, f32[256,128]{1,0:T(8,128)S(1)}, f32[256,128]{1,0:T(8,128)S(1)}) custom-call(bf16[1024,1024]{1,0:T(8,128)(2,1)} %x_hbm.1, bf16[1024,128]{1,0:T(8,128)(2,1)} %b_hbm.1, bf16[1024,128]{1,0:T(8,128)(2,1)} %c_hbm.1, bf16[1024,1024]{1,0:T(8,128)(2,1)} %d_hbm.1, ...), custom_call_target="tpu_custom_call" | custom-call | tf_op jit(solution)/shard_map/pallas_call | solution.py:482
  43.8 2.1 %shard_map.94 = (bf16[1024,1024]{1,0:T(8,128)(2,1)}, bf16[1024,1024]{1,0:T(8,128)(2,1)}, f32[256,128]{1,0:T(8,128)}, f32[256,128]{1,0:T(8,128)}) custom-call(bf16[1024,1024]{1,0:T(8,128)(2,1)S(1)} %get-tuple-element.8.refs_0_, bf16[1024,1024]{1,0:T(8,128)(2,1)S(1)} %get-tuple-element.9.refs_1_, f32[256,128]{1,0:T(8,128)S(1)} %get-tuple-element.10.refs_2_, ...), custom_call_target="tpu_custom_call" | custom-call | tf_op jit(solution)/shard_map/pallas_call | solution.py:537
